TPU v7x, 512 devices: a whole 4x8x8 slice. The times are simulated.
512 devices in a mesh: dp: 16 (over y, core), tensor: 32 (over x, z).
Axes of the slice: x: 4, y: 8, z: 8, core: 2. Of those that a mesh axis runs over, the one named last changes fastest.
Arguments:
- tokens: bfloat16 [32768, 2048], P(('dp', 'tensor')), may hold values from -6 to 6
- norm_gain: bfloat16 [2048], replicated, may hold values from 0.25 to 1.75
- query_weight: bfloat16 [2048, 2048], P('dp'), may hold values from -0.125 to 0.125
- keyval_weight: bfloat16 [2, 2048, 512], P(None, 'dp'), may hold values from -0.125 to 0.125
- query_gain: float32 [64], replicated, may hold values from 0.5 to 2
- key_gain: float32 [64], replicated, may hold values from 0.5 to 2
- output_weight: bfloat16 [2048, 2048], P(None, 'dp'), may hold values from -0.75 to 0.75
- keyval_cache: bfloat16 [512, 2048, 128], P(('dp', 'tensor')), may hold values from -96 to 96
- cached_lengths: int32 [64], P('dp'), may hold values from 1 to 2048, as said below
- sink_count: int32 [64], P('dp'), may hold values from 1 to 32
- window: int32 [64], P('dp'), may hold values from 512 to 4096, as said below
Outputs:
- attended: bfloat16 [32768, 2048], P(('dp', 'tensor'))
- fresh_keyvals: bfloat16 [512, 512, 128], P(('dp', 'tensor'))
Inputs may be any that keep to these rules, and one draw needn't show every extreme that they name: `cached_lengths`: some request has exactly 2048 cached tokens. Some request has a window of exactly 4096.
All inputs are finite; a program needn't handle non-finite values.
Results may differ from a plain program's by a relative error of at most 0.014.
The roundings to bfloat16 on the way count: a program that leaves them out, or rounds other values in their place, can miss the bound.
Values may be sent and summed in bfloat16 or wider, within the bound.
A program may use at most 64 MiB of HBM per device.

v0:
```python
import jax
import jax.numpy as jnp
from jax import lax
from jax.sharding import PartitionSpec as P

epsilon = 1e-05
theta_base = 1000000.0
key_block = 1024
query_block = 512


def from_partner(block, axis, apart):
    count = lax.axis_size(axis)
    route = []
    for low in range(count):
        high = low | 1 << apart
        if high != low and high < count:
            route += [(low, high), (high, low)]
    return lax.ppermute(block, axis, route)


def rms_scale(values, weights):
    mean_square = jnp.mean(values * values, axis=-1, keepdims=True)
    return values * lax.rsqrt(mean_square + epsilon) * weights


def rotate(values, positions):
    half_dim = values.shape[-1] // 2
    inverse_freq = theta_base ** (-2.0 * jnp.arange(half_dim, dtype=jnp.float32) / values.shape[-1])
    angles = positions.astype(jnp.float32)[:, None] * inverse_freq[None, :]
    cosine = jnp.cos(angles)
    sine_part = jnp.sin(angles)
    first_half = values[..., :half_dim]
    second_half = values[..., half_dim:]
    return jnp.concatenate(
        [
            first_half * cosine - second_half * sine_part,
            second_half * cosine + first_half * sine_part,
        ],
        axis=-1,
    )


def ordered_pair(mine, partner, upper_side, axis_index):
    return jnp.where(
        upper_side,
        jnp.concatenate([partner, mine], axis=axis_index),
        jnp.concatenate([mine, partner], axis=axis_index),
    )


def body(
    tokens,
    norm_gain,
    query_weight,
    keyval_weight,
    query_gain,
    key_gain,
    output_weight,
    keyval_cache,
    cached_lengths,
    sink_count,
    window,
):
    tensor_rank = lax.axis_index("tensor")
    head_dim = query_gain.shape[0]
    kv_heads = keyval_weight.shape[2] // head_dim
    group_bits = kv_heads.bit_length() - 1
    member = tensor_rank % kv_heads
    request_slot = tensor_rank // kv_heads
    length = cached_lengths[request_slot]
    sink_total = sink_count[request_slot]
    window_len = window[request_slot]
    block_cols = query_weight.shape[1] // kv_heads
    head_count = block_cols // head_dim
    new_rows = tokens.shape[0] * kv_heads

    def bit_set(bit_index):
        return tensor_rank // 2**bit_index % 2 == 1

    normed = rms_scale(tokens.astype(jnp.float32), norm_gain.astype(jnp.float32)).astype(
        jnp.bfloat16
    )
    gathered = normed
    for bit_index in range(group_bits):
        partner = from_partner(gathered, "tensor", bit_index)
        gathered = ordered_pair(gathered, partner, bit_set(bit_index), 0)
    query_local = lax.dynamic_slice_in_dim(query_weight, member * block_cols, block_cols, 1)
    keyval_local = lax.dynamic_slice_in_dim(keyval_weight, member * head_dim, head_dim, 2)
    combined = jnp.concatenate([query_local, keyval_local[0], keyval_local[1]], axis=1)
    projected = jnp.dot(
        gathered,
        lax.all_gather(combined, "dp", axis=0, tiled=True),
        preferred_element_type=jnp.float32,
    )
    query_raw = projected[:, :block_cols].reshape(new_rows, head_count, head_dim).transpose(1, 0, 2)
    key_raw = projected[:, block_cols : block_cols + head_dim]
    value_new = projected[:, block_cols + head_dim :].astype(jnp.bfloat16)
    positions = length + jnp.arange(new_rows, dtype=jnp.int32)
    queries = rotate(rms_scale(query_raw, query_gain), positions).astype(jnp.bfloat16)
    key_new = rotate(rms_scale(key_raw, key_gain), positions).astype(jnp.bfloat16)
    fresh = jnp.concatenate([key_new, value_new], axis=1)[None]
    cache_rows = keyval_cache[0]
    cache_slots = cache_rows.shape[0]
    all_keys = jnp.concatenate([cache_rows[:, :head_dim], key_new], axis=0)
    all_values = jnp.concatenate([cache_rows[:, head_dim:], value_new], axis=0)
    slot_pos = jnp.arange(cache_slots, dtype=jnp.int32)
    key_pos = jnp.concatenate([slot_pos, positions])
    key_live = jnp.concatenate([slot_pos < length, jnp.ones((new_rows,), jnp.bool_)])
    total_keys = all_keys.shape[0]
    bounds = [
        (block_low, min(block_low + key_block, total_keys))
        for block_low in range(0, total_keys, key_block)
    ]
    scale = head_dim ** (-0.5)
    flat_rows = head_count * new_rows
    flat_pos = jnp.tile(positions, head_count).reshape(flat_rows // query_block, query_block)

    def allowed_in(query_pos, block_low, block_high):
        block_pos = key_pos[block_low:block_high][None, :]
        block_live = key_live[block_low:block_high][None, :]
        return (
            block_live
            & (block_pos <= query_pos[:, None])
            & ((block_pos < sink_total) | (query_pos[:, None] - block_pos < window_len))
        )

    def attend(operands):
        block_queries, query_pos = operands
        masked_blocks = []
        for block_low, block_high in bounds:
            allowed = allowed_in(query_pos, block_low, block_high)

            def score_block(unused, block_low=block_low, block_high=block_high, allowed=allowed):
                scores = (
                    jnp.einsum(
                        "qd,kd->qk",
                        block_queries,
                        all_keys[block_low:block_high],
                        preferred_element_type=jnp.float32,
                    )
                    * scale
                )
                return jnp.where(allowed, scores, -jnp.inf)

            masked = score_block(0)
            masked_blocks.append((allowed, masked))
        row_max = jnp.full((query_block,), -jnp.inf, jnp.float32)
        for allowed, masked in masked_blocks:
            row_max = jnp.maximum(row_max, jnp.max(masked, axis=1))
        running = jnp.zeros((query_block,), jnp.float32)
        accum = jnp.zeros((query_block, head_dim), jnp.float32)
        for (block_low, block_high), (allowed, masked) in zip(bounds, masked_blocks):

            def add_block(
                carried, block_low=block_low, block_high=block_high, allowed=allowed, masked=masked
            ):
                weights = jnp.where(allowed, jnp.exp(masked - row_max[:, None]), 0.0)
                return (
                    carried[0] + jnp.sum(weights, axis=1),
                    carried[1]
                    + jnp.dot(
                        weights.astype(jnp.bfloat16),
                        all_values[block_low:block_high],
                        preferred_element_type=jnp.float32,
                    ),
                )

            running, accum = add_block((running, accum))
        return (accum / running[:, None]).astype(jnp.bfloat16)

    outputs = lax.map(attend, (queries, flat_pos))
    head_out = (
        outputs.reshape(head_count, new_rows, head_dim)
        .transpose(1, 0, 2)
        .reshape(new_rows, block_cols)
    )
    out_rows = lax.dynamic_slice_in_dim(output_weight, member * block_cols, block_cols, 0)
    current = jnp.dot(
        head_out,
        lax.all_gather(out_rows, "dp", axis=1, tiled=True),
        preferred_element_type=jnp.float32,
    )
    for bit_index in reversed(range(group_bits)):
        half = current.shape[0] // 2
        upper_side = bit_set(bit_index)
        keep = jnp.where(upper_side, current[half:], current[:half])
        send = jnp.where(upper_side, current[:half], current[half:])
        current = keep + from_partner(send.astype(jnp.bfloat16), "tensor", bit_index).astype(
            send.dtype
        )
    attended = current.astype(jnp.bfloat16)
    return (attended, fresh)


def solution(mesh):
    in_specs = (
        P(("dp", "tensor"), None),
        P(),
        P("dp", None),
        P(None, "dp", None),
        P(),
        P(),
        P(None, "dp"),
        P(("dp", "tensor"), None, None),
        P("dp"),
        P("dp"),
        P("dp"),
    )
    out_specs = (P(("dp", "tensor"), None), P(("dp", "tensor"), None, None))
    return jax.shard_map(body, mesh=mesh, in_specs=in_specs, out_specs=out_specs, check_vma=False)
```

profile of v0, /device:TPU:1, one launch (start us, length us, event | category | flops | bytes accessed | tf_op | source)
XLA Modules:
  0.0 271.1 jit_solution(11251175954020895935)
XLA Ops:
  12.9 4.8 %collective-permute-start = (bf16[64,2048]{1,0:T(8,128)(2,1)S(1)}, bf16[64,2048]{1,0:T(8,128)(2,1)S(1)}, u32[]{:S(2)}, u32[]{:S(2)}) collective-permute-start(bf16[64,2048]{1,0:T(8,128)(2,1)S(1)} %fusion.66), channel_id=1, source_target_pairs={{0,1},{1,0},{2,3},{3,2},{4,5},{5,4},{6,7},{7,6},{8,9},{9,8},{10,11... | collective-permute-start | bytes 786440 | tf_op jit(solution)/shard_map/ppermute | solution.py:19
  17.7 3.7 %collective-permute-done = bf16[64,2048]{1,0:T(8,128)(2,1)S(1)} collective-permute-done((bf16[64,2048]{1,0:T(8,128)(2,1)S(1)}, bf16[64,2048]{1,0:T(8,128)(2,1)S(1)}, u32[]{:S(2)}, u32[]{:S(2)}) %collective-permute-start) | collective-permute-done | bytes 262176 | tf_op jit(solution)/shard_map/ppermute | solution.py:19
  21.6 8.1 %collective-permute-start.1 = (bf16[128,2048]{1,0:T(8,128)(2,1)S(1)}, bf16[128,2048]{1,0:T(8,128)(2,1)S(1)}, u32[]{:S(2)}, u32[]{:S(2)}) collective-permute-start(bf16[128,2048]{1,0:T(8,128)(2,1)S(1)} %maximum_select_fusion.3), channel_id=1, source_target_pairs={{0,2},{2,0},{1,3},{3,1},{4,6},{6,4},{5,7},{7,5},{8,10},{10,8},{9,1... | collective-permute-start | bytes 1572872 | tf_op jit(solution)/shard_map/ppermute | solution.py:19
  29.7 22.8 %collective-permute-done.1 = bf16[128,2048]{1,0:T(8,128)(2,1)S(1)} collective-permute-done((bf16[128,2048]{1,0:T(8,128)(2,1)S(1)}, bf16[128,2048]{1,0:T(8,128)(2,1)S(1)}, u32[]{:S(2)}, u32[]{:S(2)}) %collective-permute-start.1) | collective-permute-done | bytes 524320 | tf_op jit(solution)/shard_map/ppermute | solution.py:19
  52.7 8.1 %collective-permute-start.2 = (bf16[256,2048]{1,0:T(8,128)(2,1)S(1)}, bf16[256,2048]{1,0:T(8,128)(2,1)}, u32[]{:S(2)}, u32[]{:S(2)}) collective-permute-start(bf16[256,2048]{1,0:T(8,128)(2,1)S(1)} %maximum_select_fusion.2), channel_id=1, source_target_pairs={{0,4},{4,0},{1,5},{5,1},{2,6},{6,2},{3,7},{7,3},{8,12},{12,8},{9,1... | collective-permute-start | bytes 3145736 | tf_op jit(solution)/shard_map/ppermute | solution.py:19
  60.8 1.5 constant_dynamic-slice_fusion.1
  67.2 38.6 %collective-permute-done.2 = bf16[256,2048]{1,0:T(8,128)(2,1)} collective-permute-done((bf16[256,2048]{1,0:T(8,128)(2,1)S(1)}, bf16[256,2048]{1,0:T(8,128)(2,1)}, u32[]{:S(2)}, u32[]{:S(2)}) %collective-permute-start.2) | collective-permute-done | bytes 1048608 | tf_op jit(solution)/shard_map/ppermute | solution.py:19
  105.8 3.1 %fusion.55 = f32[512,384]{0,1:T(8,128)S(1)} fusion(bf16[2048,384]{1,0:T(8,128)(2,1)} %all-gather.3.cloned.1.call-done, bf16[256,2048]{1,0:T(8,128)(2,1)S(1)} %maximum_select_fusion.2, bf16[256,2048]{1,0:T(8,128)(2,1)} %collective-permute-done.2, pred[]{:T(512)S(6)} %eq.22), kind=kOutput, calls=%fused_computation.67 | convolution fusion | flops 814743552 | bytes 4456449 | tf_op jit(solution)/shard_map/dot_general | solution.py:91
  114.0 65.8 %while.12 = (s32[]{:T(128)}, bf16[4,512,64]{1,2,0:T(8,128)(2,1)S(1)}, pred[2048]{0:T(1024)(128)(4,1)S(1)}, s32[2048]{0:T(1024)S(1)}, s32[4,512]{1,0:T(4,128)S(1)...) while((s32[]{:T(128)}, ...), condition=%wide.region_10.11_spmd.clone.clone, body=%wide.region_3.10_spmd.clone.clone.sunk | while | flops 374475264 | bytes 20781308 | solution.py:172
  115.0 2.6 fusion.108
  120.8 3.2 %fusion.111 = (f32[512]{0:T(512)S(1)}, f32[512]{0:T(512)S(1)}) fusion(f32[512,1024]{1,0:T(8,128)S(1)} %get-tuple-element.317, f32[512]{0:T(512)S(1)} %maximum_maximum_fusion.2, s32[]{:T(128)} %get-tuple-element.355, pred[1024]{0:T(1024)(128)(4,1)S(1)} %get-tuple-element.309, s32[512]{0:T(512)S(1)} %bitcast.61, s32[1024]{0:T(1024)S(1)} %get-tuple-element.310, ...), kind=kLoop, calls=%fused_computation.17.clone.1 | loop fusion | flops 11533312 | bytes 4214788 | tf_op jit(solution)/shard_map/while/body/eval_jaxpr/reduce_sum | solution.py:160
  125.2 1.9 fusion.109
  127.1 2.0 convolution_add_fusion.3
  131.5 2.6 fusion.108
  137.2 3.2 %fusion.111 = (f32[512]{0:T(512)S(1)}, f32[512]{0:T(512)S(1)}) fusion(f32[512,1024]{1,0:T(8,128)S(1)} %get-tuple-element.317, f32[512]{0:T(512)S(1)} %maximum_maximum_fusion.2, s32[]{:T(128)} %get-tuple-element.355, pred[1024]{0:T(1024)(128)(4,1)S(1)} %get-tuple-element.309, s32[512]{0:T(512)S(1)} %bitcast.61, s32[1024]{0:T(1024)S(1)} %get-tuple-element.310, ...), kind=kLoop, calls=%fused_computation.17.clone.1 | loop fusion | flops 11533312 | bytes 4214788 | tf_op jit(solution)/shard_map/while/body/eval_jaxpr/reduce_sum | solution.py:160
  141.7 1.9 fusion.109
  143.6 2.0 convolution_add_fusion.3
  147.9 2.6 fusion.108
  153.7 3.2 %fusion.111 = (f32[512]{0:T(512)S(1)}, f32[512]{0:T(512)S(1)}) fusion(f32[512,1024]{1,0:T(8,128)S(1)} %get-tuple-element.317, f32[512]{0:T(512)S(1)} %maximum_maximum_fusion.2, s32[]{:T(128)} %get-tuple-element.355, pred[1024]{0:T(1024)(128)(4,1)S(1)} %get-tuple-element.309, s32[512]{0:T(512)S(1)} %bitcast.61, s32[1024]{0:T(1024)S(1)} %get-tuple-element.310, ...), kind=kLoop, calls=%fused_computation.17.clone.1 | loop fusion | flops 11533312 | bytes 4214788 | tf_op jit(solution)/shard_map/while/body/eval_jaxpr/reduce_sum | solution.py:160
  158.1 1.9 fusion.109
  160.1 2.0 convolution_add_fusion.3
  164.4 2.6 fusion.108
  170.2 3.2 %fusion.111 = (f32[512]{0:T(512)S(1)}, f32[512]{0:T(512)S(1)}) fusion(f32[512,1024]{1,0:T(8,128)S(1)} %get-tuple-element.317, f32[512]{0:T(512)S(1)} %maximum_maximum_fusion.2, s32[]{:T(128)} %get-tuple-element.355, pred[1024]{0:T(1024)(128)(4,1)S(1)} %get-tuple-element.309, s32[512]{0:T(512)S(1)} %bitcast.61, s32[1024]{0:T(1024)S(1)} %get-tuple-element.310, ...), kind=kLoop, calls=%fused_computation.17.clone.1 | loop fusion | flops 11533312 | bytes 4214788 | tf_op jit(solution)/shard_map/while/body/eval_jaxpr/reduce_sum | solution.py:160
  174.6 1.9 fusion.109
  176.5 2.0 convolution_add_fusion.3
  179.8 2.0 fusion.73
  182.0 4.2 %collective-permute-start.3 = (bf16[256,2048]{1,0:T(8,128)(2,1)S(1)}, bf16[256,2048]{1,0:T(8,128)(2,1)S(1)}, u32[]{:S(2)}, u32[]{:S(2)}) collective-permute-start(bf16[256,2048]{1,0:T(8,128)(2,1)S(1)} %select_convert_fusion), channel_id=1, source_target_pairs={{0,4},{4,0},{1,5},{5,1},{2,6},{6,2},{3,7},{7,3},{8,12},{12,8},{9,1... | collective-permute-start | bytes 3145736 | tf_op jit(solution)/shard_map/ppermute | solution.py:19
  186.2 40.9 %collective-permute-done.3 = bf16[256,2048]{1,0:T(8,128)(2,1)S(1)} collective-permute-done((bf16[256,2048]{1,0:T(8,128)(2,1)S(1)}, bf16[256,2048]{1,0:T(8,128)(2,1)S(1)}, u32[]{:S(2)}, u32[]{:S(2)}) %collective-permute-start.3) | collective-permute-done | bytes 1048608 | tf_op jit(solution)/shard_map/ppermute | solution.py:19
  227.8 1.9 collective-permute-start.4
  229.8 25.1 %collective-permute-done.4 = bf16[128,2048]{1,0:T(8,128)(2,1)S(1)} collective-permute-done((bf16[128,2048]{1,0:T(8,128)(2,1)S(1)}, bf16[128,2048]{1,0:T(8,128)(2,1)S(1)}, u32[]{:S(2)}, u32[]{:S(2)}) %collective-permute-start.4) | collective-permute-done | bytes 524320 | tf_op jit(solution)/shard_map/ppermute | solution.py:19
  255.1 1.9 collective-permute-start.5
  257.8 5.6 %collective-permute-done.5 = bf16[64,2048]{1,0:T(8,128)(2,1)S(1)} collective-permute-done((bf16[64,2048]{1,0:T(8,128)(2,1)S(1)}, bf16[64,2048]{1,0:T(8,128)(2,1)S(1)}, u32[]{:S(2)}, u32[]{:S(2)}) %collective-permute-start.5) | collective-permute-done | bytes 262176 | tf_op jit(solution)/shard_map/ppermute | solution.py:19
  (126 shorter events, 45.1 us)
Async XLA Ops:
  7.2 1.0 copy-start
  7.2 98.6 %all-gather.3.cloned.1.call-start = ((), (), s32[]{:S(2)}) async-start(), calls=%async_computation | async-start | bytes 1671168 | tf_op jit(solution)/shard_map/all_gather | solution.py:93
  9.8 170.0 %all-gather.5.cloned.1.call-start = ((), (), s32[]{:S(2)}) async-start(), calls=%async_computation.1 | async-start | bytes 1114112 | tf_op jit(solution)/shard_map/all_gather | solution.py:181
  10.6 51.8 %copy-start.7 = (s32[4]{0:T(128)S(1)}, s32[4]{0:T(128)}, u32[]{:S(2)}) copy-start(s32[4]{0:T(128)} %param.21) | copy-start | bytes 52
  10.6 52.4 %copy-start.8 = (s32[4]{0:T(128)S(1)}, s32[4]{0:T(128)}, u32[]{:S(2)}) copy-start(s32[4]{0:T(128)} %param.22) | copy-start | bytes 52
  10.6 53.0 %copy-start.9 = (s32[4]{0:T(128)S(1)}, s32[4]{0:T(128)}, u32[]{:S(2)}) copy-start(s32[4]{0:T(128)} %param.23) | copy-start | bytes 52
  10.6 55.6 %copy-start.1 = (bf16[1,2048,128]{2,1,0:T(8,128)(2,1)S(1)}, bf16[1,2048,128]{2,1,0:T(8,128)(2,1)}, u32[]{:S(2)}) copy-start(bf16[1,2048,128]{2,1,0:T(8,128)(2,1)} %param.20) | copy-start | bytes 1572868
  12.9 8.6 %collective-permute-start = (bf16[64,2048]{1,0:T(8,128)(2,1)S(1)}, bf16[64,2048]{1,0:T(8,128)(2,1)S(1)}, u32[]{:S(2)}, u32[]{:S(2)}) collective-permute-start(bf16[64,2048]{1,0:T(8,128)(2,1)S(1)} %fusion.66), channel_id=1, source_target_pairs={{0,1},{1,0},{2,3},{3,2},{4,5},{5,4},{6,7},{7,6},{8,9},{9,8},{10,11... | collective-permute-start | bytes 786440 | tf_op jit(solution)/shard_map/ppermute | solution.py:19
  21.6 30.9 %collective-permute-start.1 = (bf16[128,2048]{1,0:T(8,128)(2,1)S(1)}, bf16[128,2048]{1,0:T(8,128)(2,1)S(1)}, u32[]{:S(2)}, u32[]{:S(2)}) collective-permute-start(bf16[128,2048]{1,0:T(8,128)(2,1)S(1)} %maximum_select_fusion.3), channel_id=1, source_target_pairs={{0,2},{2,0},{1,3},{3,1},{4,6},{6,4},{5,7},{7,5},{8,10},{10,8},{9,1... | collective-permute-start | bytes 1572872 | tf_op jit(solution)/shard_map/ppermute | solution.py:19
  52.7 53.1 %collective-permute-start.2 = (bf16[256,2048]{1,0:T(8,128)(2,1)S(1)}, bf16[256,2048]{1,0:T(8,128)(2,1)}, u32[]{:S(2)}, u32[]{:S(2)}) collective-permute-start(bf16[256,2048]{1,0:T(8,128)(2,1)S(1)} %maximum_select_fusion.2), channel_id=1, source_target_pairs={{0,4},{4,0},{1,5},{5,1},{2,6},{6,2},{3,7},{7,3},{8,12},{12,8},{9,1... | collective-permute-start | bytes 3145736 | tf_op jit(solution)/shard_map/ppermute | solution.py:19
  67.2 41.8 %copy-start.5 = (f32[64]{0:T(128)S(1)}, f32[64]{0:T(128)}, u32[]{:S(2)}) copy-start(f32[64]{0:T(128)} %param.18) | copy-start | bytes 772
  109.1 3.5 %copy-start.6 = (f32[64]{0:T(128)S(1)}, f32[64]{0:T(128)}, u32[]{:S(2)}) copy-start(f32[64]{0:T(128)} %param.17) | copy-start | bytes 772
  112.9 1.0 copy-start.2
  115.0 4.5 %copy-start.3 = (bf16[512,64]{1,0:T(8,128)(2,1)S(1)}, bf16[512,64]{1,0:T(8,128)(2,1)}, u32[]{:S(2)}) copy-start(bf16[512,64]{1,0:T(8,128)(2,1)} %get-tuple-element.358) | copy-start | bytes 196612 | tf_op jit(solution)/shard_map/while
  127.1 2.0 copy-start.4
  131.5 4.5 %copy-start.3 = (bf16[512,64]{1,0:T(8,128)(2,1)S(1)}, bf16[512,64]{1,0:T(8,128)(2,1)}, u32[]{:S(2)}) copy-start(bf16[512,64]{1,0:T(8,128)(2,1)} %get-tuple-element.358) | copy-start | bytes 196612 | tf_op jit(solution)/shard_map/while
  143.6 2.0 copy-start.4
  147.9 4.5 %copy-start.3 = (bf16[512,64]{1,0:T(8,128)(2,1)S(1)}, bf16[512,64]{1,0:T(8,128)(2,1)}, u32[]{:S(2)}) copy-start(bf16[512,64]{1,0:T(8,128)(2,1)} %get-tuple-element.358) | copy-start | bytes 196612 | tf_op jit(solution)/shard_map/while
  160.0 2.0 copy-start.4
  164.4 4.5 %copy-start.3 = (bf16[512,64]{1,0:T(8,128)(2,1)S(1)}, bf16[512,64]{1,0:T(8,128)(2,1)}, u32[]{:S(2)}) copy-start(bf16[512,64]{1,0:T(8,128)(2,1)} %get-tuple-element.358) | copy-start | bytes 196612 | tf_op jit(solution)/shard_map/while
  176.5 2.0 copy-start.4
  182.0 45.1 %collective-permute-start.3 = (bf16[256,2048]{1,0:T(8,128)(2,1)S(1)}, bf16[256,2048]{1,0:T(8,128)(2,1)S(1)}, u32[]{:S(2)}, u32[]{:S(2)}) collective-permute-start(bf16[256,2048]{1,0:T(8,128)(2,1)S(1)} %select_convert_fusion), channel_id=1, source_target_pairs={{0,4},{4,0},{1,5},{5,1},{2,6},{6,2},{3,7},{7,3},{8,12},{12,8},{9,1... | collective-permute-start | bytes 3145736 | tf_op jit(solution)/shard_map/ppermute | solution.py:19
  227.8 27.0 %collective-permute-start.4 = (bf16[128,2048]{1,0:T(8,128)(2,1)S(1)}, bf16[128,2048]{1,0:T(8,128)(2,1)S(1)}, u32[]{:S(2)}, u32[]{:S(2)}) collective-permute-start(bf16[128,2048]{1,0:T(8,128)(2,1)S(1)} %select_convert_fusion.1), channel_id=1, source_target_pairs={{0,2},{2,0},{1,3},{3,1},{4,6},{6,4},{5,7},{7,5},{8,10},{10,8},{9,1... | collective-permute-start | bytes 1572872 | tf_op jit(solution)/shard_map/ppermute | solution.py:19
  255.1 8.4 %collective-permute-start.5 = (bf16[64,2048]{1,0:T(8,128)(2,1)S(1)}, bf16[64,2048]{1,0:T(8,128)(2,1)S(1)}, u32[]{:S(2)}, u32[]{:S(2)}) collective-permute-start(bf16[64,2048]{1,0:T(8,128)(2,1)S(1)} %select_convert_fusion.2), channel_id=1, source_target_pairs={{0,1},{1,0},{2,3},{3,2},{4,5},{5,4},{6,7},{7,6},{8,9},{9,8},{10,11... | collective-permute-start | bytes 786440 | tf_op jit(solution)/shard_map/ppermute | solution.py:19
Sparse Core Ops, SparseCore 0:
  10.7 47.3 all-gather.2
  62.4 40.4 all-gather.4
where the time goes:
time: 273 us; the launch traced here: 271 us
  waiting for transfers between devices  137 us (50%)
  matrix products  42.5 us (16%)
  other arithmetic  38.1 us (14%)
  starting transfers between devices  29.1 us (11%)
  between operations  14.5 us (5%)
  local copies, waits for them, and re-layouts  9.56 us (4%)
    ppermute x6, waiting for transfers between devices, from_partner(): return lax.ppermute(block, axis, route)  137 us
    ppermute x6, starting transfers between devices, from_partner(): return lax.ppermute(block, axis, route)  29.1 us
    dot_general x12, matrix products, add_block(): jnp.dot(weights.astype(jnp.bfloat16), all_values[block_low:block_high], p...  20.7 us
    reduce_sum x8, other arithmetic, add_block(): jnp.sum(weights, axis=1)  17.6 us
    dot_general x12, matrix products, score_block(): jnp.einsum('qd,kd->qk', block_queries, all_keys[block_low:block_high], pr...  16.8 us
    lt x8, other arithmetic, allowed_in(): block_pos < sink_total  7.36 us
  transfers between devices with their start and end apart: 8, of which 6 were waited for; matrix products, arithmetic and copies ran while one was open for 31% of the time, Pallas kernels for 0%

commit v1 on v0

v1 whole, which is shorter than its diff:
```python
import functools

import jax
import jax.numpy as jnp
import numpy as np
from jax import lax
from jax.experimental import pallas as pl
from jax.experimental.pallas import tpu as pltpu
from jax.sharding import PartitionSpec as P

MESH = pl.DeviceIdType.MESH
F32, BF16 = jnp.float32, jnp.bfloat16
epsilon = 1e-05
theta_base = 1000000.0
RING = 8
XS = 4
HD = 64
GROUP = 4
ROWS = 64
NEW = RING * ROWS
CACHE = 2048
D = 2048
QROWS = GROUP * ROWS
SHARD = 128
COLS = 384
KEYS = 512
STAGES = 7
SCALE = float(HD**-0.5 * np.log2(np.e))


def hop_of(stage):
    return stage // 2 + 1 if stage < 6 else 4


def part_of(stage, side):
    return stage % 2 if stage < 6 else side


def next_stage(stage, side):
    if stage <= 3:
        return stage + 2
    return 6 if stage == 4 + side else None


def kernel(
    tokens,
    norm_gain,
    query_weight,
    keyval_weight,
    query_gain,
    key_gain,
    output_weight,
    cache,
    inverse_freq,
    lengths,
    sinks,
    windows,
    out_ref,
    fresh_ref,
    tok,
    w,
    kv_pair,
    wo,
    kc,
    vc,
    new_vc,
    queries,
    accs,
    tops,
    s_ref,
    head_send,
    head_in,
    cos_t,
    sin_t,
    local_sem,
    tok_send,
    tok_recv,
    w_send,
    w_recv,
    wsib_send,
    wsib_recv,
    wo_send,
    wo_recv,
    x_send,
    x_recv,
    wosib_send,
    wosib_recv,
    head_send_sem,
    head_recv_sem,
):
    dp = lax.axis_index("dp")
    rank = lax.axis_index("tensor")
    y, core = dp // 2, dp % 2
    x, z = rank // RING, rank % RING
    parity = x % 2

    def wrap(value, size):
        return (value + size) % size

    def on_z(where):
        return (dp, x * RING + where)

    z_to = [on_z(wrap(z + 1, RING)), on_z(wrap(z - 1, RING))]
    y_to = [(wrap(y + 1, RING) * 2 + core, rank), (wrap(y - 1, RING) * 2 + core, rank)]
    x_to = [(dp, wrap(x + 1, XS) * RING + z), (dp, wrap(x - 1, XS) * RING + z)]
    sibling = (y * 2 + 1 - core, rank)
    step_back = [-1, 1]

    barrier = pltpu.get_barrier_semaphore()
    for apart in range(1, RING):
        pl.semaphore_signal(
            barrier, inc=1, device_id=on_z(wrap(z + apart, RING)), device_id_type=MESH
        )
    for other in y_to + x_to + [sibling]:
        pl.semaphore_signal(barrier, inc=1, device_id=other, device_id_type=MESH)

    def remote(src, dst, send_sem, recv_sem, device):
        return pltpu.make_async_remote_copy(
            src_ref=src,
            dst_ref=dst,
            send_sem=send_sem,
            recv_sem=recv_sem,
            device_id=device,
            device_id_type=MESH,
        )

    own_rows = pl.ds(pl.multiple_of(dp * SHARD, SHARD), SHARD)
    own_cols = pl.ds(pl.multiple_of(dp * SHARD, SHARD), SHARD)
    locals_ = [
        pltpu.make_async_copy(
            query_weight.at[:, pl.ds(pl.multiple_of(z * 256, 256), 256)],
            w.at[own_rows, pl.ds(0, 256)],
            local_sem.at[0],
        ),
        pltpu.make_async_copy(
            keyval_weight.at[:, :, pl.ds(pl.multiple_of(z // 2 * 128, 128), 128)],
            kv_pair,
            local_sem.at[1],
        ),
        pltpu.make_async_copy(cache.at[0], kc, local_sem.at[2]),
        pltpu.make_async_copy(
            tokens, tok.at[pl.ds(pl.multiple_of(z * ROWS, ROWS), ROWS)], local_sem.at[3]
        ),
        pltpu.make_async_copy(output_weight, wo.at[:, own_cols], local_sem.at[4]),
    ]
    for copy in locals_:
        copy.start()

    lane = lax.broadcasted_iota(jnp.int32, (1, 128), 1)
    low = lane < HD

    locals_[1].wait()
    odd = z % 2 == 1
    pair = kv_pair[...].astype(F32)
    key_cols = jnp.where(odd, pltpu.roll(pair[0], HD, 1), pair[0])
    value_cols = jnp.where(odd, pair[1], pltpu.roll(pair[1], HD, 1))
    w[own_rows, 256:384] = jnp.where(low, key_cols, value_cols).astype(BF16)
    locals_[0].wait()

    pl.semaphore_wait(barrier, RING - 1 + 5)

    def tok_rows(block, part):
        return pl.ds(pl.multiple_of(block * ROWS + part * 32, 32), 32)

    def tok_copy(side, stage, block, src=None):
        rows = tok_rows(block, part_of(stage, side))
        return remote(
            tok.at[rows] if src is None else src,
            tok.at[rows],
            tok_send.at[side],
            tok_recv.at[side, stage],
            z_to[side],
        )

    def tok_pump(stage):
        for side in range(2):
            block = wrap(z + step_back[side] * hop_of(stage), RING)
            tok_copy(side, stage, block).wait_recv()
            later = next_stage(stage, side)
            if later is not None:
                tok_copy(side, later, block).start()

    def w_rows(shard, part):
        return pl.ds(pl.multiple_of(shard * SHARD + part * 64, 64), 64)

    def w_copy(side, stage, shard):
        rows = w_rows(shard, part_of(stage, side))
        return remote(
            w.at[rows], w.at[rows], w_send.at[side], w_recv.at[side, stage], y_to[side]
        )

    def w_pump(stage):
        for side in range(2):
            shard = wrap(y + step_back[side] * hop_of(stage), RING) * 2 + core
            w_copy(side, stage, shard).wait_recv()
            later = next_stage(stage, side)
            if later is not None:
                w_copy(side, later, shard).start()
            rows = w_rows(shard, part_of(stage, side))
            remote(w.at[rows], w.at[rows], wsib_send, wsib_recv, sibling).start()

    def wo_part(shard, first, count):
        return (
            pl.ds(pl.multiple_of(first, 256), count),
            pl.ds(pl.multiple_of(shard * SHARD, SHARD), SHARD),
        )

    def wo_copy(side, stage, shard, from_input=False):
        first = parity * 1024 + part_of(stage, side) * 512
        rows, cols = wo_part(shard, first, 512)
        return remote(
            output_weight.at[rows] if from_input else wo.at[rows, cols],
            wo.at[rows, cols],
            wo_send.at[side],
            wo_recv.at[side, stage],
            y_to[side],
        )

    def wo_sibling(rows, cols):
        remote(wo.at[rows, cols], wo.at[rows, cols], wosib_send, wosib_recv, sibling).start()

    def wo_pump(stage):
        for side in range(2):
            shard = wrap(y + step_back[side] * hop_of(stage), RING) * 2 + core
            wo_copy(side, stage, shard).wait_recv()
            later = next_stage(stage, side)
            if later is not None:
                wo_copy(side, later, shard).start()
            first = parity * 1024 + part_of(stage, side) * 512
            for towards in range(2):
                rows, cols = wo_part(shard, first + towards * 256, 256)
                remote(
                    wo.at[rows, cols],
                    wo.at[rows, cols],
                    x_send.at[towards],
                    x_recv.at[towards, stage],
                    x_to[towards],
                ).start()
            wo_sibling(*wo_part(shard, first, 512))

    def x_pump(stage):
        for towards in range(2):
            both = wo.at[0:512, 0:128]
            remote(
                both, both, x_send.at[towards], x_recv.at[towards, stage], x_to[towards]
            ).wait_recv()
            for side in range(2):
                shard = wrap(y + step_back[side] * hop_of(stage), RING) * 2 + core
                first = (1 - parity) * 1024 + part_of(stage, side) * 512
                wo_sibling(*wo_part(shard, first + towards * 256, 256))

    for stage in range(2):
        for side in range(2):
            w_copy(side, stage, dp).start()
    for stage in range(2):
        for side in range(2):
            tok_copy(side, stage, z, tokens.at[pl.ds(stage * 32, 32)]).start()
    remote(w.at[own_rows], w.at[own_rows], wsib_send, wsib_recv, sibling).start()
    remote(output_weight, wo.at[:, own_cols], wosib_send, wosib_recv, sibling).start()

    length = lengths[x]
    sink_total = sinks[x]
    window = windows[x]
    angle_lane = lax.broadcasted_iota(jnp.int32, (NEW, 128), 1)
    position = (lax.broadcasted_iota(jnp.int32, (NEW, 128), 0) + length).astype(F32)
    angles = position * inverse_freq[...]
    cos_t[...] = jnp.cos(angles)
    sine = jnp.sin(angles)
    sin_t[...] = jnp.where(angle_lane % HD < HD // 2, -sine, sine)

    w_pump(0)
    w_pump(1)
    locals_[2].wait()
    vc[...] = jnp.where(low, jnp.ones((), BF16), kc[...])
    w_pump(2)
    tok_pump(0)
    w_pump(3)
    tok_pump(1)
    w_pump(4)
    w_pump(5)
    for stage in range(2):
        for side in range(2):
            wo_copy(side, stage, dp, True).start()
    w_pump(6)
    locals_[3].wait()
    half_w = w.at[0 : D // 2]
    remote(half_w, half_w, wsib_send, wsib_recv, sibling).wait_recv()

    slot = lax.broadcasted_iota(jnp.int32, (1, CACHE), 1)
    far = 1 << 20
    slot_pos = jnp.where(slot < length, jnp.where(slot < sink_total, far, slot), -far)
    row_token = lax.broadcasted_iota(jnp.int32, (QROWS, 1), 0) % ROWS

    same_head = (
        lax.broadcasted_iota(jnp.int32, (128, 128), 0) // HD
        == lax.broadcasted_iota(jnp.int32, (128, 128), 1) // HD
    )
    averaging = jnp.where(same_head, 1.0 / HD, 0.0).astype(BF16)
    gain = norm_gain[...].astype(F32)
    gain_q = jnp.concatenate([query_gain[...], query_gain[...]], axis=1)
    gain_k = jnp.concatenate([key_gain[...], key_gain[...]], axis=1)
    first_half = lane % HD < HD // 2

    def normed_rotated(tile, gains, cosine, sine):
        square = tile * tile
        upper = square.astype(BF16)
        lower = (square - upper.astype(F32)).astype(BF16)
        mean = jnp.dot(upper, averaging, preferred_element_type=F32) + jnp.dot(
            lower, averaging, preferred_element_type=F32
        )
        scaled = tile * lax.rsqrt(mean + epsilon) * gains
        swapped = jnp.where(
            first_half, pltpu.roll(scaled, 128 - HD // 2, 1), pltpu.roll(scaled, HD // 2, 1)
        )
        return scaled * cosine + swapped * sine

    def project(block):
        rows = pl.ds(pl.multiple_of(block * ROWS, ROWS), ROWS)
        values = tok[rows].astype(F32)
        mean = jnp.mean(values * values, axis=1, keepdims=True)
        normed = (values * lax.rsqrt(mean + epsilon) * gain).astype(BF16)
        raw = jnp.dot(normed, w[...], preferred_element_type=F32)
        cosine, sine = cos_t[rows], sin_t[rows]
        query_rows = pl.multiple_of(block * QROWS, QROWS)
        for pair_index in range(2):
            tile = normed_rotated(
                raw[:, pair_index * 128 : pair_index * 128 + 128], gain_q, cosine, sine
            )
            for odd_head in range(2):
                head = jnp.where(low, pltpu.roll(tile, HD, 1) if odd_head else tile, 0.0)
                at = query_rows + (pair_index * 2 + odd_head) * ROWS
                queries[pl.ds(pl.multiple_of(at, ROWS), ROWS)] = head.astype(BF16)
        last = raw[:, 256:384]
        keyval = jnp.where(low, normed_rotated(last, gain_k, cosine, sine), last).astype(BF16)
        fresh_ref[0, rows] = keyval
        new_vc[rows] = jnp.where(low, jnp.ones((), BF16), keyval)

    def scores_of(block_queries, keys):
        return lax.dot_general(
            block_queries, keys, (((1,), (1,)), ((), ())), preferred_element_type=F32
        )

    def attend_cache(block):
        rows = pl.ds(pl.multiple_of(block * QROWS, QROWS), QROWS)
        block_queries = queries[rows]
        oldest = length + block * ROWS + row_token - window
        top = None
        for low_key in range(0, CACHE, KEYS):
            keys = pl.ds(low_key, KEYS)
            scores = scores_of(block_queries, kc[keys])
            scores = jnp.where(slot_pos[:, low_key : low_key + KEYS] > oldest, scores, -jnp.inf)
            s_ref[:, keys] = scores
            for part in range(0, KEYS, 128):
                piece = scores[:, part : part + 128]
                top = piece if top is None else jnp.maximum(top, piece)
        top = jnp.max(top, axis=1, keepdims=True)
        acc = jnp.zeros((QROWS, 128), F32)
        for low_key in range(0, CACHE, KEYS):
            keys = pl.ds(low_key, KEYS)
            weights = jnp.exp2((s_ref[:, keys] - top) * SCALE).astype(BF16)
            acc = acc + jnp.dot(weights, vc[keys], preferred_element_type=F32)
        accs[rows] = acc
        tops[rows] = jnp.broadcast_to(top, (QROWS, 128))

    new_slot = lax.broadcasted_iota(jnp.int32, (1, NEW), 1)

    def finish(block):
        rows = pl.ds(pl.multiple_of(block * QROWS, QROWS), QROWS)
        scores = scores_of(queries[rows], fresh_ref[0])
        scores = jnp.where(new_slot <= block * ROWS + row_token, scores, -jnp.inf)
        old_top = tops[rows][:, :1]
        top = jnp.maximum(old_top, jnp.max(scores, axis=1, keepdims=True))
        weights = jnp.exp2((scores - top) * SCALE).astype(BF16)
        acc = accs[rows] * jnp.exp2((old_top - top) * SCALE) + jnp.dot(
            weights, new_vc[...], preferred_element_type=F32
        )
        mixed = acc / pltpu.roll(acc, HD, 1)
        tiles = []
        for pair_index in range(2):
            even = mixed[pair_index * 128 : pair_index * 128 + ROWS]
            odd_one = mixed[pair_index * 128 + ROWS : pair_index * 128 + 128]
            tiles.append(jnp.where(low, pltpu.roll(even, HD, 1), odd_one).astype(BF16))
        return tiles

    def block_at(order):
        hop = (order + 1) // 2
        return wrap(z + jnp.where(order % 2 == 1, -hop, hop), RING)

    def one_block(order, unused):
        for stage in range(2, STAGES):
            pl.when(order == stage - 1)(functools.partial(tok_pump, stage))
        for stage in range(4):
            pl.when(order == stage + 3)(functools.partial(wo_pump, stage))
        for stage in range(2):
            pl.when(order == stage + 5)(functools.partial(x_pump, stage))
        block = block_at(order)
        project(block)
        attend_cache(block)
        return unused

    lax.fori_loop(0, RING, one_block, 0)

    own_head = pl.ds(pl.multiple_of(z * 256, 256), 256)

    def head_copy(block):
        rows = pl.ds(pl.multiple_of(block * ROWS, ROWS), ROWS)
        return remote(
            head_send.at[rows], head_in.at[:, own_head], head_send_sem, head_recv_sem, on_z(block)
        )

    def finish_block(index, unused):
        order = RING - 1 - index
        block = block_at(order)
        tiles = finish(block)
        rows = pl.ds(pl.multiple_of(block * ROWS, ROWS), ROWS)
        for pair_index in range(2):
            head_send[rows, pair_index * 128 : pair_index * 128 + 128] = tiles[pair_index]

        @pl.when(order < RING - 1)
        def _():
            head_copy(block_at(order + 1)).start()

        return unused

    lax.fori_loop(0, RING, finish_block, 0)
    head_in[:, own_head] = head_send[pl.ds(pl.multiple_of(z * ROWS, ROWS), ROWS)]
    for stage in range(4, STAGES):
        wo_pump(stage)
        x_pump(stage - 2)
    x_pump(5)
    x_pump(6)
    locals_[4].wait()
    half_wo = wo.at[:, 0 : D // 2]
    remote(half_wo, half_wo, wosib_send, wosib_recv, sibling).wait_recv()
    heads = head_in.at[:, 0 : D - 256]
    remote(heads, heads, head_send_sem, head_recv_sem, sibling).wait_recv()

    def out_cols(index, unused):
        cols = pl.ds(pl.multiple_of(index * 256, 256), 256)
        out_ref[:, cols] = jnp.dot(
            head_in[...], wo[:, cols], preferred_element_type=F32
        ).astype(BF16)
        return unused

    lax.fori_loop(0, D // 256, out_cols, 0)

    for side in range(2):
        sent = tok.at[0:224]
        remote(sent, sent, tok_send.at[side], tok_recv.at[0, 0], z_to[side]).wait_send()
        sent = w.at[0:448]
        remote(sent, sent, w_send.at[side], w_recv.at[0, 0], y_to[side]).wait_send()
        sent = wo.at[0:1792, 0:256]
        remote(sent, sent, wo_send.at[side], wo_recv.at[0, 0], y_to[side]).wait_send()
        remote(sent, sent, x_send.at[side], x_recv.at[0, 0], x_to[side]).wait_send()
    remote(half_w, half_w, wsib_send, wsib_recv, sibling).wait_send()
    remote(half_wo, half_wo, wosib_send, wosib_recv, sibling).wait_send()
    sent = head_send.at[0:448]
    remote(sent, sent, head_send_sem, head_recv_sem, sibling).wait_send()


def body(
    tokens,
    norm_gain,
    query_weight,
    keyval_weight,
    query_gain,
    key_gain,
    output_weight,
    keyval_cache,
    cached_lengths,
    sink_count,
    window,
):
    frequency = theta_base ** (-2.0 * np.arange(HD // 2) / HD)
    inverse_freq = jnp.asarray(np.tile(frequency, 4)[None], F32)
    anywhere = pl.BlockSpec(memory_space=pl.ANY)
    vmem = pl.BlockSpec(memory_space=pltpu.VMEM)
    smem = pl.BlockSpec(memory_space=pltpu.SMEM)
    dma = pltpu.SemaphoreType.DMA
    return pl.pallas_call(
        kernel,
        out_shape=(
            jax.ShapeDtypeStruct((ROWS, D), BF16),
            jax.ShapeDtypeStruct((1, NEW, 2 * HD), BF16),
        ),
        in_specs=[anywhere, vmem, anywhere, anywhere, vmem, vmem, anywhere, anywhere, vmem]
        + [smem] * 3,
        out_specs=(vmem, vmem),
        scratch_shapes=[
            pltpu.VMEM((NEW, D), BF16),
            pltpu.VMEM((D, COLS), BF16),
            pltpu.VMEM((2, SHARD, 128), BF16),
            pltpu.VMEM((D, D), BF16),
            pltpu.VMEM((CACHE, 128), BF16),
            pltpu.VMEM((CACHE, 128), BF16),
            pltpu.VMEM((NEW, 128), BF16),
            pltpu.VMEM((RING * QROWS, 128), BF16),
            pltpu.VMEM((RING * QROWS, 128), F32),
            pltpu.VMEM((RING * QROWS, 128), F32),
            pltpu.VMEM((QROWS, CACHE), F32),
            pltpu.VMEM((NEW, 256), BF16),
            pltpu.VMEM((ROWS, D), BF16),
            pltpu.VMEM((NEW, 128), F32),
            pltpu.VMEM((NEW, 128), F32),
            dma((5,)),
            dma((2,)),
            dma((2, STAGES)),
            dma((2,)),
            dma((2, STAGES)),
            dma(()),
            dma(()),
            dma((2,)),
            dma((2, STAGES)),
            dma((2,)),
            dma((2, STAGES)),
            dma(()),
            dma(()),
            dma(()),
            dma(()),
        ],
        compiler_params=pltpu.CompilerParams(
            collective_id=0, has_side_effects=True, vmem_limit_bytes=60 << 20
        ),
        name="prefill",
    )(
        tokens,
        norm_gain.reshape(1, D),
        query_weight,
        keyval_weight,
        query_gain.reshape(1, HD),
        key_gain.reshape(1, HD),
        output_weight,
        keyval_cache,
        inverse_freq,
        cached_lengths,
        sink_count,
        window,
    )


def solution(mesh):
    in_specs = (
        P(("dp", "tensor"), None),
        P(),
        P("dp", None),
        P(None, "dp", None),
        P(),
        P(),
        P(None, "dp"),
        P(("dp", "tensor"), None, None),
        P("dp"),
        P("dp"),
        P("dp"),
    )
    out_specs = (P(("dp", "tensor"), None), P(("dp", "tensor"), None, None))
    return jax.shard_map(body, mesh=mesh, in_specs=in_specs, out_specs=out_specs, check_vma=False)
```

time: 273 us -> 78.8 us (0.29)
  waiting for transfers between devices: 137 us -> 0 us
  Pallas kernels: 0 us -> 74.3 us
  matrix products: 42.5 us -> 0 us
  other arithmetic: 38.1 us -> 0 us
  starting transfers between devices: 29.1 us -> 0 us
  between operations: 14.5 us -> 0.65 us
  local copies, waits for them, and re-layouts: 9.56 us -> 3.66 us
    ppermute x6 -> x0, waiting for transfers between devices: 137 us -> none  [from_partner(): return lax.ppermute(block, axis, route)]
    pallas_call x0 -> x1, Pallas kernels: none -> 74.3 us  [body(): pl.pallas_call(kernel, out_shape=(jax.ShapeDtypeStruct((ROWS, D), BF16),...]
    dot_general x26 -> x0, matrix products: 42.5 us -> none  [the longest x12 20.7 us: add_block(): jnp.dot(weights.astype(jnp.bfloat16), all_values[block_low:block_high], p...]
    ppermute x6 -> x0, starting transfers between devices: 29.1 us -> none  [from_partner(): return lax.ppermute(block, axis, route)]
    reduce_sum x11 -> x0, other arithmetic: 19.2 us -> none  [the longest x8 17.6 us: add_block(): jnp.sum(weights, axis=1)]
    lt x9 -> x0, other arithmetic: 8.03 us -> none  [the longest x8 7.36 us: allowed_in(): block_pos < sink_total]
    add x11 -> x0, other arithmetic: 4.19 us -> none  [the longest x5 3.38 us: body(): positions = length + jnp.arange(new_rows, dtype=jnp.int32)]
    dynamic_slice x9 -> x0, local copies, waits for them, and re-layouts: 3.43 us -> none  [the longest x1 1.48 us: body(): lax.dynamic_slice_in_dim(output_weight, member * block_cols, block_cols, 0)]
  transfers between devices with their start and end apart: 8 -> 0, of which waited for: 6 -> 0; matrix products, arithmetic and copies ran while one was open for 31% -> 0% of each run, Pallas kernels for 0% -> 0%
where the time goes in v1:
time: 78.8 us; the launch traced here: 78.6 us
  Pallas kernels  74.3 us (94%)
  local copies, waits for them, and re-layouts  3.66 us (5%)
    pallas_call x1, Pallas kernels, body(): pl.pallas_call(kernel, out_shape=(jax.ShapeDtypeStruct((ROWS, D), BF16),...  74.3 us
    unnamed x4, local copies, waits for them, and re-layouts  2.36 us

profile of v1, /device:TPU:1, one launch (start us, length us, event | category | flops | bytes accessed | tf_op | source)
XLA Modules:
  0.0 78.6 jit_solution(6867015735597487249)
XLA Ops:
  0.6 1.3 %reshape.13.norm_gain = bf16[1,2048]{1,0:T(2,128)(2,1)} reshape(bf16[2048]{0:T(1024)(128)(2,1)} %param.13) | data formatting | bytes 8192 | tf_op jit(solution)/shard_map/reshape | solution.py:527
  1.9 74.3 %prefill.1 = (bf16[64,2048]{1,0:T(8,128)(2,1)}, bf16[1,512,128]{2,1,0:T(8,128)(2,1)}) custom-call(bf16[64,2048]{1,0:T(8,128)(2,1)} %tokens.1, bf16[1,2048]{1,0:T(2,128)(2,1)} %reshape.13.norm_gain, bf16[128,2048]{1,0:T(8,128)(2,1)} %query_weight.1, bf16[2,128,512]{2,1,0:T(8,128)(2,1)} %keyval_weight.1, f32[1,64]{1,0:T(1,128)} %bitcast.2, f32[1,64]{1,0:T(1,128)} %bitcast.3, ...), custom_call_target="tpu_custom_call" | custom-call | tf_op jit(solution)/shard_map/prefill/pallas_call | solution.py:480
  76.2 0.0 copy-start
  76.3 1.7 %copy.16 = bf16[64,2048]{1,0:T(8,128)(2,1)} copy(bf16[64,2048]{1,0:T(8,128)(2,1)} %get-tuple-element.4) | data formatting | bytes 524288
  78.0 0.0 copy-done
  78.0 0.7 copy.17
Async XLA Ops:
  76.2 1.7 %copy-start = (bf16[1,512,128]{2,1,0:T(8,128)(2,1)S(1)}, bf16[1,512,128]{2,1,0:T(8,128)(2,1)}, u32[]{:S(2)}) copy-start(bf16[1,512,128]{2,1,0:T(8,128)(2,1)} %get-tuple-element.5) | copy-start | bytes 393220

commit v2 on v1

--- a/solution.py
+++ b/solution.py
@@ -24,22 +24,29 @@
 SHARD = 128
 COLS = 384
 KEYS = 512
-STAGES = 7
+PARTS = 4
+STAGES = 3 * PARTS + PARTS // 2
+TOK_PART = ROWS // PARTS
+WO_PART = 1024 // PARTS
+OFFSETS = ((4,), (3, 5), (2, 6), (1, 7))
 SCALE = float(HD**-0.5 * np.log2(np.e))
 
 
 def hop_of(stage):
-    return stage // 2 + 1 if stage < 6 else 4
+    return stage // PARTS + 1 if stage < 3 * PARTS else 4
 
 
 def part_of(stage, side):
-    return stage % 2 if stage < 6 else side
+    return stage % PARTS if stage < 3 * PARTS else stage - 3 * PARTS + side * (PARTS // 2)
 
 
 def next_stage(stage, side):
-    if stage <= 3:
-        return stage + 2
-    return 6 if stage == 4 + side else None
+    if stage < 2 * PARTS:
+        return stage + PARTS
+    part = stage - 2 * PARTS
+    if part < PARTS and part // (PARTS // 2) == side:
+        return 3 * PARTS + part - side * (PARTS // 2)
+    return None
 
 
 def kernel(
@@ -77,6 +84,8 @@
     tok_recv,
     w_send,
     w_recv,
+    wx_send,
+    wx_recv,
     wsib_send,
     wsib_recv,
     wo_send,
@@ -102,6 +111,7 @@
 
     z_to = [on_z(wrap(z + 1, RING)), on_z(wrap(z - 1, RING))]
     y_to = [(wrap(y + 1, RING) * 2 + core, rank), (wrap(y - 1, RING) * 2 + core, rank)]
+    on_y = [(wrap(y + apart, RING) * 2 + core, rank) for apart in range(1, RING)]
     x_to = [(dp, wrap(x + 1, XS) * RING + z), (dp, wrap(x - 1, XS) * RING + z)]
     sibling = (y * 2 + 1 - core, rank)
     step_back = [-1, 1]
@@ -111,7 +121,7 @@
         pl.semaphore_signal(
             barrier, inc=1, device_id=on_z(wrap(z + apart, RING)), device_id_type=MESH
         )
-    for other in y_to + x_to + [sibling]:
+    for other in on_y + x_to + [sibling]:
         pl.semaphore_signal(barrier, inc=1, device_id=other, device_id_type=MESH)
 
     def remote(src, dst, send_sem, recv_sem, device):
@@ -157,10 +167,10 @@
     w[own_rows, 256:384] = jnp.where(low, key_cols, value_cols).astype(BF16)
     locals_[0].wait()
 
-    pl.semaphore_wait(barrier, RING - 1 + 5)
+    pl.semaphore_wait(barrier, 2 * (RING - 1) + 3)
 
     def tok_rows(block, part):
-        return pl.ds(pl.multiple_of(block * ROWS + part * 32, 32), 32)
+        return pl.ds(pl.multiple_of(block * ROWS + part * TOK_PART, TOK_PART), TOK_PART)
 
     def tok_copy(side, stage, block, src=None):
         rows = tok_rows(block, part_of(stage, side))
@@ -180,34 +190,51 @@
             if later is not None:
                 tok_copy(side, later, block).start()
 
-    def w_rows(shard, part):
-        return pl.ds(pl.multiple_of(shard * SHARD + part * 64, 64), 64)
-
-    def w_copy(side, stage, shard):
-        rows = w_rows(shard, part_of(stage, side))
+    def w_rows(shard, first, count):
+        return w.at[pl.ds(pl.multiple_of(shard * SHARD + first, 32), count)]
+
+    def y_shard(offset):
+        return wrap(y + offset, RING) * 2 + core
+
+    def w_copy(offset):
+        rows = w_rows(dp, parity * 64, 64)
         return remote(
-            w.at[rows], w.at[rows], w_send.at[side], w_recv.at[side, stage], y_to[side]
-        )
-
-    def w_pump(stage):
-        for side in range(2):
-            shard = wrap(y + step_back[side] * hop_of(stage), RING) * 2 + core
-            w_copy(side, stage, shard).wait_recv()
-            later = next_stage(stage, side)
-            if later is not None:
-                w_copy(side, later, shard).start()
-            rows = w_rows(shard, part_of(stage, side))
-            remote(w.at[rows], w.at[rows], wsib_send, wsib_recv, sibling).start()
+            rows, rows, w_send, w_recv.at[offset - 1], (y_shard(offset), rank)
+        )
+
+    def w_sibling(rows):
+        remote(rows, rows, wsib_send, wsib_recv, sibling).start()
+
+    def w_pump(group):
+        for offset in OFFSETS[group]:
+            shard = y_shard(-offset)
+            rows = w_rows(shard, parity * 64, 64)
+            remote(rows, rows, w_send, w_recv.at[offset - 1], sibling).wait_recv()
+            for towards in range(2):
+                part = w_rows(shard, parity * 64 + towards * 32, 32)
+                remote(
+                    part, part, wx_send.at[towards], wx_recv.at[towards, group], x_to[towards]
+                ).start()
+            w_sibling(rows)
+
+    def wx_pump(group):
+        for towards in range(2):
+            both = w.at[0 : 32 * len(OFFSETS[group])]
+            remote(
+                both, both, wx_send.at[towards], wx_recv.at[towards, group], x_to[towards]
+            ).wait_recv()
+            for offset in OFFSETS[group]:
+                w_sibling(w_rows(y_shard(-offset), (1 - parity) * 64 + towards * 32, 32))
 
     def wo_part(shard, first, count):
         return (
-            pl.ds(pl.multiple_of(first, 256), count),
+            pl.ds(pl.multiple_of(first, 128), count),
             pl.ds(pl.multiple_of(shard * SHARD, SHARD), SHARD),
         )
 
     def wo_copy(side, stage, shard, from_input=False):
-        first = parity * 1024 + part_of(stage, side) * 512
-        rows, cols = wo_part(shard, first, 512)
+        first = parity * 1024 + part_of(stage, side) * WO_PART
+        rows, cols = wo_part(shard, first, WO_PART)
         return remote(
             output_weight.at[rows] if from_input else wo.at[rows, cols],
             wo.at[rows, cols],
@@ -219,43 +246,51 @@
     def wo_sibling(rows, cols):
         remote(wo.at[rows, cols], wo.at[rows, cols], wosib_send, wosib_recv, sibling).start()
 
-    def wo_pump(stage):
+    half = WO_PART // 2
+
+    def wo_pump(pair):
+        for stage in (2 * pair, 2 * pair + 1):
+            for side in range(2):
+                shard = y_shard(step_back[side] * hop_of(stage))
+                wo_copy(side, stage, shard).wait_recv()
+                later = next_stage(stage, side)
+                if later is not None:
+                    wo_copy(side, later, shard).start()
+                first = parity * 1024 + part_of(stage, side) * WO_PART
+                for towards in range(2):
+                    rows, cols = wo_part(shard, first + towards * half, half)
+                    remote(
+                        wo.at[rows, cols],
+                        wo.at[rows, cols],
+                        x_send.at[towards],
+                        x_recv.at[towards, pair],
+                        x_to[towards],
+                    ).start()
+                wo_sibling(*wo_part(shard, first, WO_PART))
+
+    def x_pump(pair):
+        for towards in range(2):
+            four = wo.at[0 : 4 * half, 0:128]
+            remote(
+                four, four, x_send.at[towards], x_recv.at[towards, pair], x_to[towards]
+            ).wait_recv()
+            for stage in (2 * pair, 2 * pair + 1):
+                for side in range(2):
+                    shard = y_shard(step_back[side] * hop_of(stage))
+                    first = (1 - parity) * 1024 + part_of(stage, side) * WO_PART
+                    wo_sibling(*wo_part(shard, first + towards * half, half))
+
+    for offsets in OFFSETS:
+        for offset in offsets:
+            w_copy(offset).start()
+    for stage in range(PARTS):
         for side in range(2):
-            shard = wrap(y + step_back[side] * hop_of(stage), RING) * 2 + core
-            wo_copy(side, stage, shard).wait_recv()
-            later = next_stage(stage, side)
-            if later is not None:
-                wo_copy(side, later, shard).start()
-            first = parity * 1024 + part_of(stage, side) * 512
-            for towards in range(2):
-                rows, cols = wo_part(shard, first + towards * 256, 256)
-                remote(
-                    wo.at[rows, cols],
-                    wo.at[rows, cols],
-                    x_send.at[towards],
-                    x_recv.at[towards, stage],
-                    x_to[towards],
-                ).start()
-            wo_sibling(*wo_part(shard, first, 512))
-
-    def x_pump(stage):
-        for towards in range(2):
-            both = wo.at[0:512, 0:128]
-            remote(
-                both, both, x_send.at[towards], x_recv.at[towards, stage], x_to[towards]
-            ).wait_recv()
-            for side in range(2):
-                shard = wrap(y + step_back[side] * hop_of(stage), RING) * 2 + core
-                first = (1 - parity) * 1024 + part_of(stage, side) * 512
-                wo_sibling(*wo_part(shard, first + towards * 256, 256))
-
-    for stage in range(2):
+            rows = pl.ds(stage * TOK_PART, TOK_PART)
+            tok_copy(side, stage, z, tokens.at[rows]).start()
+    w_sibling(w.at[own_rows])
+    for stage in range(PARTS):
         for side in range(2):
-            w_copy(side, stage, dp).start()
-    for stage in range(2):
-        for side in range(2):
-            tok_copy(side, stage, z, tokens.at[pl.ds(stage * 32, 32)]).start()
-    remote(w.at[own_rows], w.at[own_rows], wsib_send, wsib_recv, sibling).start()
+            wo_copy(side, stage, dp, True).start()
     remote(output_weight, wo.at[:, own_cols], wosib_send, wosib_recv, sibling).start()
 
     length = lengths[x]
@@ -268,20 +303,22 @@
     sine = jnp.sin(angles)
     sin_t[...] = jnp.where(angle_lane % HD < HD // 2, -sine, sine)
 
-    w_pump(0)
-    w_pump(1)
     locals_[2].wait()
     vc[...] = jnp.where(low, jnp.ones((), BF16), kc[...])
+    tok_pump(0)
+    w_pump(0)
+    tok_pump(1)
+    w_pump(1)
+    tok_pump(2)
     w_pump(2)
-    tok_pump(0)
+    tok_pump(3)
     w_pump(3)
-    tok_pump(1)
-    w_pump(4)
-    w_pump(5)
-    for stage in range(2):
-        for side in range(2):
-            wo_copy(side, stage, dp, True).start()
-    w_pump(6)
+    wx_pump(0)
+    wx_pump(1)
+    tok_pump(4)
+    wx_pump(2)
+    tok_pump(5)
+    wx_pump(3)
     locals_[3].wait()
     half_w = w.at[0 : D // 2]
     remote(half_w, half_w, wsib_send, wsib_recv, sibling).wait_recv()
@@ -386,15 +423,35 @@
         hop = (order + 1) // 2
         return wrap(z + jnp.where(order % 2 == 1, -hop, hop), RING)
 
+    plan = {
+        0: [(tok_pump, 6)],
+        2: [(tok_pump, 7)],
+        3: [(tok_pump, 8), (wo_pump, 0)],
+        5: [(tok_pump, 9)],
+        6: [(tok_pump, 10), (wo_pump, 1), (x_pump, 0)],
+        8: [(tok_pump, 11)],
+        9: [(tok_pump, 12), (wo_pump, 2), (x_pump, 1)],
+        11: [(tok_pump, 13)],
+        12: [(wo_pump, 3), (x_pump, 2)],
+        15: [(wo_pump, 4), (x_pump, 3)],
+        18: [(wo_pump, 5), (x_pump, 4)],
+        21: [(wo_pump, 6), (x_pump, 5)],
+    }
+
+    def run_plan(place, first, last, stride):
+        for at, steps in plan.items():
+            if first <= at < last and (at - first) % stride == 0:
+
+                @pl.when(place == at)
+                def _(steps=steps):
+                    for pump, which in steps:
+                        pump(which)
+
     def one_block(order, unused):
-        for stage in range(2, STAGES):
-            pl.when(order == stage - 1)(functools.partial(tok_pump, stage))
-        for stage in range(4):
-            pl.when(order == stage + 3)(functools.partial(wo_pump, stage))
-        for stage in range(2):
-            pl.when(order == stage + 5)(functools.partial(x_pump, stage))
         block = block_at(order)
+        run_plan(order * 2, 0, 2 * RING, 2)
         project(block)
+        run_plan(order * 2 + 1, 1, 2 * RING, 2)
         attend_cache(block)
         return unused
 
@@ -411,6 +468,7 @@
     def finish_block(index, unused):
         order = RING - 1 - index
         block = block_at(order)
+        run_plan(2 * RING + index, 2 * RING, 3 * RING, 1)
         tiles = finish(block)
         rows = pl.ds(pl.multiple_of(block * ROWS, ROWS), ROWS)
         for pair_index in range(2):
@@ -424,10 +482,6 @@
 
     lax.fori_loop(0, RING, finish_block, 0)
     head_in[:, own_head] = head_send[pl.ds(pl.multiple_of(z * ROWS, ROWS), ROWS)]
-    for stage in range(4, STAGES):
-        wo_pump(stage)
-        x_pump(stage - 2)
-    x_pump(5)
     x_pump(6)
     locals_[4].wait()
     half_wo = wo.at[:, 0 : D // 2]
@@ -447,11 +501,13 @@
     for side in range(2):
         sent = tok.at[0:224]
         remote(sent, sent, tok_send.at[side], tok_recv.at[0, 0], z_to[side]).wait_send()
-        sent = w.at[0:448]
-        remote(sent, sent, w_send.at[side], w_recv.at[0, 0], y_to[side]).wait_send()
+        sent = w.at[0:224]
+        remote(sent, sent, wx_send.at[side], wx_recv.at[0, 0], x_to[side]).wait_send()
         sent = wo.at[0:1792, 0:256]
         remote(sent, sent, wo_send.at[side], wo_recv.at[0, 0], y_to[side]).wait_send()
         remote(sent, sent, x_send.at[side], x_recv.at[0, 0], x_to[side]).wait_send()
+    sent = w.at[0:448]
+    remote(sent, sent, w_send, w_recv.at[0], sibling).wait_send()
     remote(half_w, half_w, wsib_send, wsib_recv, sibling).wait_send()
     remote(half_wo, half_wo, wosib_send, wosib_recv, sibling).wait_send()
     sent = head_send.at[0:448]
@@ -505,14 +561,16 @@
             dma((5,)),
             dma((2,)),
             dma((2, STAGES)),
+            dma(()),
+            dma((RING - 1,)),
             dma((2,)),
-            dma((2, STAGES)),
+            dma((2, len(OFFSETS))),
             dma(()),
             dma(()),
             dma((2,)),
             dma((2, STAGES)),
             dma((2,)),
-            dma((2, STAGES)),
+            dma((2, STAGES // 2)),
             dma(()),
             dma(()),
             dma(()),

time: 78.8 us -> 72.4 us (0.919)
  Pallas kernels: 74.3 us -> 67.9 us
    pallas_call x1, Pallas kernels: 74.3 us -> 67.9 us  [body(): pl.pallas_call(kernel, out_shape=(jax.ShapeDtypeStruct((ROWS, D), BF16),...]
where the time goes in v2:
time: 72.4 us; the launch traced here: 72.2 us
  Pallas kernels  67.9 us (94%)
  local copies, waits for them, and re-layouts  3.66 us (5%)
    pallas_call x1, Pallas kernels, body(): pl.pallas_call(kernel, out_shape=(jax.ShapeDtypeStruct((ROWS, D), BF16),...  67.9 us
    unnamed x4, local copies, waits for them, and re-layouts  2.36 us

profile of v2, /device:TPU:1, one launch (start us, length us, event | category | flops | bytes accessed | tf_op | source)
XLA Modules:
  0.0 72.2 jit_solution(10723460721300094856)
XLA Ops:
  0.6 1.3 %reshape.13.norm_gain = bf16[1,2048]{1,0:T(2,128)(2,1)} reshape(bf16[2048]{0:T(1024)(128)(2,1)} %param.13) | data formatting | bytes 8192 | tf_op jit(solution)/shard_map/reshape | solution.py:585
  1.9 67.9 %prefill.1 = (bf16[64,2048]{1,0:T(8,128)(2,1)}, bf16[1,512,128]{2,1,0:T(8,128)(2,1)}) custom-call(bf16[64,2048]{1,0:T(8,128)(2,1)} %tokens.1, bf16[1,2048]{1,0:T(2,128)(2,1)} %reshape.13.norm_gain, bf16[128,2048]{1,0:T(8,128)(2,1)} %query_weight.1, bf16[2,128,512]{2,1,0:T(8,128)(2,1)} %keyval_weight.1, f32[1,64]{1,0:T(1,128)} %bitcast.2, f32[1,64]{1,0:T(1,128)} %bitcast.3, ...), custom_call_target="tpu_custom_call" | custom-call | tf_op jit(solution)/shard_map/prefill/pallas_call | solution.py:536
  69.8 0.0 copy-start
  69.8 1.7 %copy.16 = bf16[64,2048]{1,0:T(8,128)(2,1)} copy(bf16[64,2048]{1,0:T(8,128)(2,1)} %get-tuple-element.4) | data formatting | bytes 524288
  71.5 0.0 copy-done
  71.5 0.7 copy.17
Async XLA Ops:
  69.8 1.7 %copy-start = (bf16[1,512,128]{2,1,0:T(8,128)(2,1)S(1)}, bf16[1,512,128]{2,1,0:T(8,128)(2,1)}, u32[]{:S(2)}) copy-start(bf16[1,512,128]{2,1,0:T(8,128)(2,1)} %get-tuple-element.5) | copy-start | bytes 393220
